TPU v7x, 32 devices: a whole 2x2x4 slice. The times are simulated.
32 devices in a mesh: dp: 8 (over z, x), seq: 4 (over y, core).
Axes of the slice: x: 2, y: 2, z: 4, core: 2. Of those that a mesh axis runs over, the one named last changes fastest.
Arguments:
- tokens: float32 [16, 256, 1024], P('dp', 'seq'), may hold values from -6 to 6
- output_cotangent: float32 [16, 256, 1024], P('dp', 'seq'), may hold values from -0.5 to 0.5
- placement: int32 [8], replicated, may hold values from 0 to 15, as said below
- inward: float32 [1024, 3072], P(('dp', 'seq'))
- outward: float32 [1024, 1024], P(('dp', 'seq')), may hold values from -0.75 to 0.75
- attend_vectors: float32 [5, 1024], P(None, ('dp', 'seq'))
- expand: float32 [1024, 4096], P(('dp', 'seq')), may hold values from -0.1875 to 0.1875
- shrink: float32 [4096, 1024], P(('dp', 'seq')), may hold values from -0.09375 to 0.09375
- feed_vectors: float32 [3, 1024], P(None, ('dp', 'seq'))
- expand_bias: float32 [4096], P(('dp', 'seq')), may hold values from -3 to 3
- inward_moments: float32 [2, 1024, 3072], P(None, ('dp', 'seq')), as said below
- outward_moments: float32 [2, 1024, 1024], P(None, ('dp', 'seq'))
- attend_moments: float32 [2, 5, 1024], P(None, None, ('dp', 'seq'))
- expand_moments: float32 [2, 1024, 4096], P(None, ('dp', 'seq'))
- shrink_moments: float32 [2, 4096, 1024], P(None, ('dp', 'seq'))
- feed_moments: float32 [2, 3, 1024], P(None, None, ('dp', 'seq'))
- bias_moments: float32 [2, 4096], P(None, ('dp', 'seq'))
Outputs:
- block_output: float32 [16, 256, 1024], P('dp', 'seq')
- input_gradient: float32 [16, 256, 1024], P('dp', 'seq')
- inward_gradient: float32 [1024, 3072], P(('dp', 'seq'))
- outward_gradient: float32 [1024, 1024], P(('dp', 'seq'))
- attend_gradient: float32 [5, 1024], P(None, ('dp', 'seq'))
- expand_gradient: float32 [1024, 4096], P(('dp', 'seq'))
- shrink_gradient: float32 [4096, 1024], P(('dp', 'seq'))
- feed_gradient: float32 [3, 1024], P(None, ('dp', 'seq'))
- bias_gradient: float32 [4096], P(('dp', 'seq'))
- inward_new: float32 [1024, 3072], P(('dp', 'seq'))
- outward_new: float32 [1024, 1024], P(('dp', 'seq'))
- attend_new: float32 [5, 1024], P(None, ('dp', 'seq'))
- expand_new: float32 [1024, 4096], P(('dp', 'seq'))
- shrink_new: float32 [4096, 1024], P(('dp', 'seq'))
- feed_new: float32 [3, 1024], P(None, ('dp', 'seq'))
- bias_new: float32 [4096], P(('dp', 'seq'))
- inward_state: float32 [2, 1024, 3072], P(None, ('dp', 'seq'))
- outward_state: float32 [2, 1024, 1024], P(None, ('dp', 'seq'))
- attend_state: float32 [2, 5, 1024], P(None, None, ('dp', 'seq'))
- expand_state: float32 [2, 1024, 4096], P(None, ('dp', 'seq'))
- shrink_state: float32 [2, 4096, 1024], P(None, ('dp', 'seq'))
- feed_state: float32 [2, 3, 1024], P(None, None, ('dp', 'seq'))
- bias_state: float32 [2, 4096], P(None, ('dp', 'seq'))
Inputs may be any that keep to these rules, and one draw needn't show every extreme that they name: `placement`: entries are distinct slot numbers; slot s belongs to index s // 2 of dp; in every draw some index of dp holds 2 sequences. `inward_moments`: the second moment (index 1) is positive.
All inputs are finite; a program needn't handle non-finite values.
Results may differ from a plain program's by a relative error of at most 0.012.
Values may be sent and summed in bfloat16 or wider, within the bound.
A program may use at most 192 MiB of HBM per device.

v0:
```python
import math
import jax
import jax.numpy as jnp
from jax import lax
from jax.sharding import PartitionSpec as P

HEADS = 16
HEAD_DIM = 64
norm_epsilon = 1e-05
beta_first = 0.9
beta_second = 0.95
adam_epsilon = 1e-08
learn_rate = 0.01
weight_decay = 0.1
adam_steps = 4
gelu_scale = 0.7978845608028654
gelu_cubic = 0.044715
masked_score = -1e30


def halved(operand):
    return operand.astype(jnp.bfloat16)


def normalize(operand):
    average = jnp.mean(operand, axis=-1, keepdims=True)
    centered = operand - average
    variance = jnp.mean(centered * centered, axis=-1, keepdims=True)
    inverse = lax.rsqrt(variance + norm_epsilon)
    return (centered * inverse, inverse)


def norm_back(upstream, normed, inverse):
    first_mean = jnp.mean(upstream, axis=-1, keepdims=True)
    second_mean = jnp.mean(upstream * normed, axis=-1, keepdims=True)
    return inverse * (upstream - first_mean - normed * second_mean)


def gelu_pair(upper):
    inner_arg = gelu_scale * (upper + gelu_cubic * upper * upper * upper)
    tangent = jnp.tanh(inner_arg)
    active = 0.5 * upper * (1.0 + tangent)
    slope = 0.5 * (1.0 + tangent) + 0.5 * upper * (1.0 - tangent * tangent) * gelu_scale * (
        1.0 + 3.0 * gelu_cubic * upper * upper
    )
    return (active, slope)


def adamw_update(parameter, gradient, moments, decay_rate):
    first_moment = beta_first * moments[0] + (1.0 - beta_first) * gradient
    second = beta_second * moments[1] + (1.0 - beta_second) * gradient * gradient
    unbiased_first = first_moment / (1.0 - beta_first**adam_steps)
    unbiased_second = second / (1.0 - beta_second**adam_steps)
    update = unbiased_first / (jnp.sqrt(unbiased_second) + adam_epsilon) + decay_rate * parameter
    return (parameter - learn_rate * update, jnp.stack([first_moment, second]))


def lifted_fold(normed, pieces):
    weight_piece, vector_piece = pieces
    vector_float = vector_piece.astype(jnp.float32)
    lift_piece = halved(normed * vector_float[:, 0] + vector_float[:, 1])
    total = jnp.dot(lift_piece, weight_piece, preferred_element_type=jnp.float32)
    return (total, lift_piece, vector_float)


def body(
    tokens,
    output_cotangent,
    placement,
    inward,
    outward,
    attend_vectors,
    expand,
    shrink,
    feed_vectors,
    expand_bias,
    inward_moments,
    outward_moments,
    attend_moments,
    expand_moments,
    shrink_moments,
    feed_moments,
    bias_moments,
):
    slot_count, block_size, model_width = tokens.shape
    length = block_size * lax.axis_size("seq")
    row_count = slot_count * block_size
    score_scale = 1.0 / math.sqrt(HEAD_DIM)
    slot_ids = lax.axis_index("dp") * slot_count + jnp.arange(slot_count, dtype=jnp.int32)
    live_mask = jnp.any(placement[None, :] == slot_ids[:, None], axis=1).astype(jnp.float32)[
        :, None, None
    ]
    flat_tokens = tokens.reshape(row_count, model_width)
    normed_one, inverse_one = normalize(flat_tokens)
    attend_cols = halved(attend_vectors).T
    feed_cols = halved(feed_vectors).T
    packed, lifted_one, vec_rows_one = lifted_fold(
        normed_one,
        (
            lax.all_gather(halved(inward), ("dp", "seq"), axis=0, tiled=True),
            lax.all_gather(attend_cols, ("dp", "seq"), axis=0, tiled=True),
        ),
    )
    vec_one = vec_rows_one.T
    queries = halved(packed[:, :model_width] + vec_one[2]).reshape(
        slot_count, block_size, HEADS, HEAD_DIM
    )
    key_local = halved(packed[:, model_width : 2 * model_width]).reshape(
        slot_count, block_size, model_width
    )
    value_local = halved(packed[:, 2 * model_width :] + vec_one[3]).reshape(
        slot_count, block_size, model_width
    )
    key_whole, value_whole = (
        lax.all_gather(key_local, "seq", axis=1, tiled=True),
        lax.all_gather(value_local, "seq", axis=1, tiled=True),
    )
    key_heads = key_whole.reshape(slot_count, length, HEADS, HEAD_DIM)
    value_heads = value_whole.reshape(slot_count, length, HEADS, HEAD_DIM)
    query_pos = lax.axis_index("seq") * block_size + jnp.arange(block_size)
    allowed = jnp.arange(length)[None, :] <= query_pos[:, None]
    scores = (
        jnp.einsum("sqhd,skhd->shqk", queries, key_heads, preferred_element_type=jnp.float32)
        * score_scale
    )
    scores = jnp.where(allowed, scores, masked_score)
    score_peak = jnp.max(scores, axis=-1, keepdims=True)
    log_total = score_peak + jnp.log(jnp.sum(jnp.exp(scores - score_peak), axis=-1, keepdims=True))
    weights_half = halved(jnp.exp(scores - log_total))
    attended = halved(
        jnp.einsum(
            "shqk,skhd->sqhd", weights_half, value_heads, preferred_element_type=jnp.float32
        ).reshape(row_count, model_width)
    )
    projected = jnp.dot(
        attended,
        lax.all_gather(halved(outward), ("dp", "seq"), axis=0, tiled=True),
        preferred_element_type=jnp.float32,
    )
    middle = flat_tokens + projected + vec_one[4]
    normed_two, inverse_two = normalize(middle)
    upper_raw, lifted_two, vec_rows_two = lifted_fold(
        normed_two,
        (
            lax.all_gather(halved(expand), ("dp", "seq"), axis=0, tiled=True),
            lax.all_gather(feed_cols, ("dp", "seq"), axis=0, tiled=True),
        ),
    )
    vec_two = vec_rows_two.T
    weight_piece = lax.all_gather(halved(shrink), ("dp", "seq"), axis=0, tiled=True)
    bias_piece = lax.all_gather(halved(expand_bias), ("dp", "seq"), axis=0, tiled=True)
    bias_float = bias_piece.astype(jnp.float32)
    upper_cols = upper_raw + bias_float
    act_cols, unused_slope = gelu_pair(upper_cols)
    act_half = halved(act_cols)
    total = jnp.dot(act_half, weight_piece, preferred_element_type=jnp.float32)
    upper_act = upper_raw + bias_float
    unused_active, gelu_slope = gelu_pair(upper_act)
    result = middle + total + vec_two[2]
    block_output = result.reshape(slot_count, block_size, model_width) * live_mask
    cotangent = (output_cotangent * live_mask).reshape(row_count, model_width)
    cot_half = halved(cotangent)
    shrink_grad = jnp.dot(act_half.T, cot_half, preferred_element_type=jnp.float32)
    feed_bias_grad = jnp.sum(cotangent, axis=0)
    upper_grad = (
        jnp.dot(
            cot_half,
            lax.all_gather(halved(shrink), ("dp", "seq"), axis=0, tiled=True).T,
            preferred_element_type=jnp.float32,
        )
        * gelu_slope
    )
    upper_half = halved(upper_grad)
    expand_grad = jnp.dot(lifted_two.T, upper_half, preferred_element_type=jnp.float32)
    expand_bias_grad = jnp.sum(upper_grad, axis=0)
    lift_two_grad = jnp.dot(
        upper_half,
        lax.all_gather(halved(expand), ("dp", "seq"), axis=0, tiled=True).T,
        preferred_element_type=jnp.float32,
    )
    gain_two_grad = jnp.sum(lift_two_grad * normed_two, axis=0)
    shift_two_grad = jnp.sum(lift_two_grad, axis=0)
    middle_grad = cotangent + norm_back(lift_two_grad * vec_two[0], normed_two, inverse_two)
    feed_vec_grad = jnp.stack([gain_two_grad, shift_two_grad, feed_bias_grad], axis=1)
    feed_parts = (
        lax.psum_scatter(expand_grad, ("dp", "seq"), scatter_dimension=0, tiled=True),
        lax.psum_scatter(shrink_grad, ("dp", "seq"), scatter_dimension=0, tiled=True),
        lax.psum_scatter(feed_vec_grad, ("dp", "seq"), scatter_dimension=0, tiled=True),
        lax.psum_scatter(expand_bias_grad, ("dp", "seq"), scatter_dimension=0, tiled=True),
    )
    middle_half = halved(middle_grad)
    outward_grad = jnp.dot(attended.T, middle_half, preferred_element_type=jnp.float32)
    out_bias_grad = jnp.sum(middle_grad, axis=0)
    attended_back = jnp.dot(
        middle_half,
        lax.all_gather(halved(outward), ("dp", "seq"), axis=0, tiled=True).T,
        preferred_element_type=jnp.float32,
    )
    attended_grad = halved(attended_back).reshape(slot_count, block_size, HEADS, HEAD_DIM)
    attended_heads = attended.reshape(slot_count, block_size, HEADS, HEAD_DIM)
    delta_sum = jnp.sum(
        attended_grad.astype(jnp.float32) * attended_heads.astype(jnp.float32), axis=-1
    )
    scores_again = (
        jnp.einsum("sqhd,skhd->shqk", queries, key_heads, preferred_element_type=jnp.float32)
        * score_scale
    )
    scores_again = jnp.where(allowed, scores_again, masked_score)
    weights_full = jnp.exp(scores_again - log_total)
    weights_again = halved(weights_full)
    weight_grad = jnp.einsum(
        "sqhd,skhd->shqk", attended_grad, value_heads, preferred_element_type=jnp.float32
    )
    score_grad = halved(
        weights_full * (weight_grad - jnp.transpose(delta_sum, (0, 2, 1))[..., None]) * score_scale
    )
    query_grad = jnp.einsum(
        "shqk,skhd->sqhd", score_grad, key_heads, preferred_element_type=jnp.float32
    ).reshape(row_count, model_width)
    key_term = jnp.einsum(
        "shqk,sqhd->skhd", score_grad, queries, preferred_element_type=jnp.float32
    ).reshape(slot_count, length, model_width)
    value_term = jnp.einsum(
        "shqk,sqhd->skhd", weights_again, attended_grad, preferred_element_type=jnp.float32
    ).reshape(slot_count, length, model_width)
    key_grad, value_grad = (
        lax.psum_scatter(
            key_term.astype(jnp.bfloat16), "seq", scatter_dimension=1, tiled=True
        ).astype(jnp.float32),
        lax.psum_scatter(
            value_term.astype(jnp.bfloat16), "seq", scatter_dimension=1, tiled=True
        ).astype(jnp.float32),
    )
    key_grad = key_grad.reshape(row_count, model_width)
    value_grad = value_grad.reshape(row_count, model_width)
    packed_grad = halved(jnp.concatenate([query_grad, key_grad, value_grad], axis=1))
    inward_grad = jnp.dot(lifted_one.T, packed_grad, preferred_element_type=jnp.float32)
    query_bias_grad = jnp.sum(query_grad, axis=0)
    value_bias_grad = jnp.sum(value_grad, axis=0)
    lift_one_grad = jnp.dot(
        packed_grad,
        lax.all_gather(halved(inward), ("dp", "seq"), axis=0, tiled=True).T,
        preferred_element_type=jnp.float32,
    )
    gain_one_grad = jnp.sum(lift_one_grad * normed_one, axis=0)
    shift_one_grad = jnp.sum(lift_one_grad, axis=0)
    tokens_grad = middle_grad + norm_back(lift_one_grad * vec_one[0], normed_one, inverse_one)
    input_gradient = tokens_grad.reshape(slot_count, block_size, model_width) * live_mask
    attend_vec_grad = jnp.stack(
        [gain_one_grad, shift_one_grad, query_bias_grad, value_bias_grad, out_bias_grad], axis=1
    )
    attend_parts = (
        lax.psum_scatter(inward_grad, ("dp", "seq"), scatter_dimension=0, tiled=True),
        lax.psum_scatter(outward_grad, ("dp", "seq"), scatter_dimension=0, tiled=True),
        lax.psum_scatter(attend_vec_grad, ("dp", "seq"), scatter_dimension=0, tiled=True),
    )
    attend_vec_sum = attend_parts[2].T
    feed_vec_sum = feed_parts[2].T
    inward_new, inward_state = adamw_update(inward, attend_parts[0], inward_moments, weight_decay)
    outward_new, outward_state = adamw_update(
        outward, attend_parts[1], outward_moments, weight_decay
    )
    attend_new, attend_state = adamw_update(attend_vectors, attend_vec_sum, attend_moments, 0.0)
    expand_new, expand_state = adamw_update(expand, feed_parts[0], expand_moments, weight_decay)
    shrink_new, shrink_state = adamw_update(shrink, feed_parts[1], shrink_moments, weight_decay)
    feed_new, feed_state = adamw_update(feed_vectors, feed_vec_sum, feed_moments, 0.0)
    bias_new, bias_state = adamw_update(expand_bias, feed_parts[3], bias_moments, 0.0)
    return (
        block_output,
        input_gradient,
        attend_parts[0],
        attend_parts[1],
        attend_vec_sum,
        feed_parts[0],
        feed_parts[1],
        feed_vec_sum,
        feed_parts[3],
        inward_new,
        outward_new,
        attend_new,
        expand_new,
        shrink_new,
        feed_new,
        bias_new,
        inward_state,
        outward_state,
        attend_state,
        expand_state,
        shrink_state,
        feed_state,
        bias_state,
    )


def solution(mesh):
    placed = (
        P("dp", "seq", None),
        P("dp", "seq", None),
        P(),
        P(("dp", "seq"), None),
        P(("dp", "seq"), None),
        P(None, ("dp", "seq")),
        P(("dp", "seq"), None),
        P(("dp", "seq"), None),
        P(None, ("dp", "seq")),
        P(("dp", "seq")),
        P(None, ("dp", "seq"), None),
        P(None, ("dp", "seq"), None),
        P(None, None, ("dp", "seq")),
        P(None, ("dp", "seq"), None),
        P(None, ("dp", "seq"), None),
        P(None, None, ("dp", "seq")),
        P(None, ("dp", "seq")),
    )
    return jax.shard_map(
        body,
        mesh=mesh,
        in_specs=placed,
        out_specs=(
            P("dp", "seq", None),
            P("dp", "seq", None),
            P(("dp", "seq"), None),
            P(("dp", "seq"), None),
            P(None, ("dp", "seq")),
            P(("dp", "seq"), None),
            P(("dp", "seq"), None),
            P(None, ("dp", "seq")),
            P(("dp", "seq")),
            P(("dp", "seq"), None),
            P(("dp", "seq"), None),
            P(None, ("dp", "seq")),
            P(("dp", "seq"), None),
            P(("dp", "seq"), None),
            P(None, ("dp", "seq")),
            P(("dp", "seq")),
            P(None, ("dp", "seq"), None),
            P(None, ("dp", "seq"), None),
            P(None, None, ("dp", "seq")),
            P(None, ("dp", "seq"), None),
            P(None, ("dp", "seq"), None),
            P(None, None, ("dp", "seq")),
            P(None, ("dp", "seq")),
        ),
        check_vma=False,
    )
```

profile of v0, /device:TPU:9, one launch (start us, length us, event | category | flops | bytes accessed | tf_op | source)
XLA Modules:
  0.0 1384.8 jit_solution(13482467230646633061)
XLA Ops:
  7.2 1.7 convert_element_type.120
  9.8 36.3 %all-gather = bf16[32,32,5]{1,2,0:T(8,128)(2,1)S(1)} all-gather(bf16[1,32,5]{1,2,0:T(8,128)(2,1)S(1)} %convert_bitcast_fusion), channel_id=1, replica_groups=mesh['dp'=8,'seq'=4] {'dp','seq'}, dimensions={0}, use_global_device_ids=true | all-gather | bytes 10560 | tf_op jit(solution)/shard_map/all_gather | solution.py:101
  46.2 1.2 reduce_sum.171
  47.4 1.2 multiply_reduce_fusion.6
  49.6 32.9 %all-gather.10.cloned.1.call-done = bf16[1024,3072]{1,0:T(8,128)(2,1)} async-done(((bf16[32,3072]{1,0:T(8,128)(2,1)}), bf16[1024,3072]{1,0:T(8,128)(2,1)}) %all-gather.10.cloned.1.call-update) | async-done | bytes 6291472 | tf_op jit(solution)/shard_map/all_gather | solution.py:100
  82.5 3.8 fusion.61
  86.3 0.8 fusion.11
  89.6 33.0 %all-gather.1 = bf16[32,32,3]{1,2,0:T(4,128)(2,1)S(1)} all-gather(bf16[1,32,3]{1,2,0:T(4,128)(2,1)S(1)} %convert_bitcast_fusion.1), channel_id=1, replica_groups=mesh['dp'=8,'seq'=4] {'dp','seq'}, dimensions={0}, use_global_device_ids=true | all-gather | bytes 6336 | tf_op jit(solution)/shard_map/all_gather | solution.py:146
  122.7 36.5 %all-gather.2 = bf16[32,1,128]{2,1,0:T(2,128)(2,1)S(1)} all-gather(bf16[1,1,128]{2,1,0:T(2,128)(2,1)S(1)} %convert_bitcast_fusion.2), channel_id=1, replica_groups=mesh['dp'=8,'seq'=4] {'dp','seq'}, dimensions={0}, use_global_device_ids=true | all-gather | bytes 8448 | tf_op jit(solution)/shard_map/all_gather | solution.py:151
  163.9 2.4 copy.101
  166.4 2.3 copy.102
  168.7 1.9 fusion.58
  172.4 1.2 copy.104
  173.6 2.1 convert_element_type.126
  175.8 4.3 all-gather.16.cloned.1.call-done
  180.1 2.2 fusion.59
  182.6 77.8 %all-gather.18.cloned.1.call-done = bf16[1024,4096]{1,0:T(8,128)(2,1)} async-done(((bf16[32,4096]{1,0:T(8,128)(2,1)}), bf16[1024,4096]{1,0:T(8,128)(2,1)}) %all-gather.18.cloned.1.call-update) | async-done | bytes 8388624 | tf_op jit(solution)/shard_map/all_gather | solution.py:145
  260.3 4.8 convolution_add_fusion
  265.1 1.3 copy-done.1
  266.5 8.1 fusion.49
  274.7 183.9 %reduce-scatter.23.cloned.1.call-done = f32[128,1024]{1,0:T(8,128)} async-done(((f32[4096,1024]{1,0:T(8,128)}), f32[128,1024]{1,0:T(8,128)}) %reduce-scatter.23.cloned.1.call-update) | async-done | bytes 524304 | tf_op jit(solution)/shard_map/reduce_scatter | solution.py:187
  458.6 3.2 fusion.24
  462.1 1.4 fusion.55
  463.5 75.1 %all-gather.20.cloned.1.call-done = bf16[4096,1024]{1,0:T(8,128)(2,1)} async-done(((bf16[128,1024]{1,0:T(8,128)(2,1)}), bf16[4096,1024]{1,0:T(8,128)(2,1)}) %all-gather.20.cloned.1.call-update) | async-done | bytes 8388624 | tf_op jit(solution)/shard_map/all_gather | solution.py:150
  538.6 8.3 fusion.60
  546.9 7.4 multiply_reduce_fusion.1
  554.3 0.8 fusion.51
  555.9 1.5 convolution_convert_fusion.3
  557.4 2.1 reshape.220
  559.6 2.2 copy.107
  561.8 2.6 convolution_convert_fusion
  564.4 2.3 copy.112
  566.7 1.4 multiply_reduce_fusion
  568.2 2.3 multiply_convert_fusion
  570.5 1.0 copy-done.5
  571.4 1.4 convolution_convert_fusion.1
  572.8 2.4 copy.110
  577.3 1.0 copy.119
  578.7 11.0 reduce-scatter.15.cloned.1.call-done
  589.6 27.4 %reduce-scatter.13.cloned.1.call-done = bf16[2,64,1024]{2,1,0:T(8,128)(2,1)} async-done(((bf16[2,256,1024]{2,1,0:T(8,128)(2,1)}), bf16[2,64,1024]{2,1,0:T(8,128)(2,1)}) %reduce-scatter.13.cloned.1.call-update) | async-done | bytes 262160 | tf_op jit(solution)/shard_map/reduce_scatter | solution.py:227
  617.0 6.1 multiply_reduce_fusion.2
  623.2 1.0 copy.117
  624.3 2.7 fusion.26
  627.2 0.9 copy-done.30
  628.0 6.3 fusion.19
  634.5 1.1 copy-done.16
  635.6 8.2 fusion.14
  644.5 2.3 pad_maximum_fusion.1
  646.8 39.5 %all-reduce = f32[4096]{0:T(1024)S(1)} all-reduce(f32[4096]{0:T(1024)S(1)} %copy-done.42), channel_id=10, replica_groups=mesh['dp'=8,'seq'=4] {'dp','seq'}, use_global_device_ids=true, to_apply=%region_29.30.clone | all-reduce | flops 4096 | bytes 32768
  687.5 5.7 fusion.8
  693.3 38.3 %reduce-scatter.27.cloned.1.call-done = f32[32,3]{1,0:T(8,128)} async-done(((f32[1024,3]{1,0:T(8,128)}), f32[32,3]{1,0:T(8,128)}) %reduce-scatter.27.cloned.1.call-update) | async-done | bytes 400
  731.6 0.8 copy.120
  733.6 1.5 multiply_add_fusion.1
  735.1 1.2 broadcast_multiply_fusion
  736.3 129.6 %reduce-scatter.25.cloned.1.call-done = f32[32,5]{1,0:T(8,128)} async-done(((f32[1024,5]{1,0:T(8,128)}), f32[32,5]{1,0:T(8,128)}) %reduce-scatter.25.cloned.1.call-update) | async-done | bytes 656
  865.9 0.8 copy.118
  867.9 138.4 %reduce-scatter.19.cloned.1.call-done = f32[32,1024]{1,0:T(8,128)} async-done(((f32[1024,1024]{1,0:T(8,128)}), f32[32,1024]{1,0:T(8,128)}) %reduce-scatter.19.cloned.1.call-update) | async-done | bytes 131088 | tf_op jit(solution)/shard_map/reduce_scatter | solution.py:254
  1006.4 1.7 fusion.33
  1008.8 176.5 %reduce-scatter.17.cloned.1.call-done = f32[32,3072]{1,0:T(8,128)} async-done(((f32[1024,3072]{1,0:T(8,128)}), f32[32,3072]{1,0:T(8,128)}) %reduce-scatter.17.cloned.1.call-update) | async-done | bytes 393232 | tf_op jit(solution)/shard_map/reduce_scatter | solution.py:253
  1185.3 2.1 fusion.31
  1187.3 0.9 pad_maximum_fusion.3
  1188.3 186.7 %reduce-scatter.21.cloned.1.call-done = f32[32,4096]{1,0:T(8,128)} async-done(((f32[1024,4096]{1,0:T(8,128)}), f32[32,4096]{1,0:T(8,128)}) %reduce-scatter.21.cloned.1.call-update) | async-done | bytes 524304 | tf_op jit(solution)/shard_map/reduce_scatter | solution.py:186
  1375.0 2.2 fusion.23
  1377.2 1.0 pad_maximum_fusion
  (206 shorter events, 19.9 us)
Async XLA Ops:
  7.2 42.2 %copy-start = (f32[2,64,1024]{2,1,0:T(8,128)S(1)}, f32[2,64,1024]{2,1,0:T(8,128)}, u32[]{:S(2)}) copy-start(f32[2,64,1024]{2,1,0:T(8,128)} %param.17) | copy-start | bytes 1572868
  7.2 75.3 %all-gather.10.cloned.1.call-start = ((), (), s32[]{:S(2)}) async-start(), calls=%async_computation.8 | async-start | bytes 6488064 | tf_op jit(solution)/shard_map/all_gather | solution.py:100
  9.0 154.9 %all-gather.12.cloned.1.call-start = ((), (), s32[]{:S(2)}) async-start(), calls=%async_computation.9 | async-start | bytes 1310720 | tf_op jit(solution)/shard_map/all_gather | solution.py:116
  47.4 2.1 copy-start.50
  86.2 1.8 copy-start.26
  86.2 2.5 copy-start.18
  86.3 3.3 copy-start.44
  86.3 36.4 %copy-start.59 = (f32[128]{0:T(128)S(1)}, f32[128]{0:T(128)}, u32[]{:S(2)}) copy-start(f32[128]{0:T(128)} %param.26) | copy-start | bytes 1540
  86.3 73.6 %copy-start.61 = (s32[8]{0:T(128)S(1)}, s32[8]{0:T(128)}, u32[]{:S(2)}) copy-start(s32[8]{0:T(128)} %param.19) | copy-start | bytes 100
  87.1 79.3 %all-gather.14.cloned.1.call-start = ((), (), s32[]{:S(2)}) async-start(), calls=%async_computation.10 | async-start | bytes 1310720 | tf_op jit(solution)/shard_map/all_gather | solution.py:115
  87.9 72.9 %copy-start.27 = (f32[2,64,1024]{2,1,0:T(8,128)S(1)}, f32[2,64,1024]{2,1,0:T(8,128)}, u32[]{:S(2)}) copy-start(f32[2,64,1024]{2,1,0:T(8,128)} %param.18) | copy-start | bytes 1572868
  87.9 92.1 %all-gather.16.cloned.1.call-start = ((), (), s32[]{:S(2)}) async-start(), calls=%async_computation.11 | async-start | bytes 2162688 | tf_op jit(solution)/shard_map/all_gather | solution.py:137
  88.7 171.7 %all-gather.18.cloned.1.call-start = ((), (), s32[]{:S(2)}) async-start(), calls=%async_computation.12 | async-start | bytes 8650752 | tf_op jit(solution)/shard_map/all_gather | solution.py:145
  89.5 369.1 %reduce-scatter.23.cloned.1.call-start = ((), (), s32[]{:S(2)}) async-start(), calls=%async_computation.19 | async-start | bytes 17301504 | tf_op jit(solution)/shard_map/reduce_scatter | solution.py:187
  122.7 43.7 %copy-start.31 = (f32[1024,3]{0,1:T(4,128)}, f32[1024,3]{0,1:T(4,128)S(1)}, u32[]{:S(2)}) copy-start(f32[1024,3]{0,1:T(4,128)S(1)} %reshape.232) | copy-start | bytes 36868
  160.1 6.3 copy-start.56
  163.9 4.8 copy-start.10
  168.7 3.2 copy-start.4
  172.4 7.7 copy-start.14
  182.3 371.9 %copy-start.32 = (f32[128]{0:T(128)}, f32[128]{0:T(128)S(1)}, u32[]{:S(2)}) copy-start(f32[128]{0:T(128)S(1)} %broadcast_multiply_fusion.8) | copy-start | bytes 1540
  182.5 82.6 %copy-start.34 = (f32[128]{0:T(128)}, f32[128]{0:T(128)S(1)}, u32[]{:S(2)}) copy-start(f32[128]{0:T(128)S(1)} %add_rsqrt_fusion.1) | copy-start | bytes 1540
  260.3 6.1 copy-start.21
  274.6 263.9 %all-gather.20.cloned.1.call-start = ((), (), s32[]{:S(2)}) async-start(), calls=%async_computation.13 | async-start | bytes 8650752 | tf_op jit(solution)/shard_map/all_gather | solution.py:150
  461.8 127.8 %reduce-scatter.15.cloned.1.call-start = ((), (), s32[]{:S(2)}) async-start(), calls=%async_computation.15 | async-start | bytes 1310720 | tf_op jit(solution)/shard_map/reduce_scatter | solution.py:230
  538.6 8.3 copy-start.35
  546.9 7.4 copy-start.15
  546.9 7.4 copy-start.13
  554.3 1.7 copy-start.9
  566.7 50.3 %reduce-scatter.13.cloned.1.call-start = ((), (), s32[]{:S(2)}) async-start(), calls=%async_computation.14 | async-start | bytes 1310720 | tf_op jit(solution)/shard_map/reduce_scatter | solution.py:227
  568.2 3.3 copy-start.11
  572.8 2.5 copy-start.3
  572.8 2.5 copy-start.6
  575.3 156.3 %reduce-scatter.27.cloned.1.call-start = ((), (), s32[]{:S(2)}) async-start(), calls=%async_computation.21 | async-start | bytes 540672
  575.8 41.2 %copy-start.37 = (f32[1,1024]{1,0:T(1,128)S(1)}, f32[1,1024]{1,0:T(1,128)}, u32[]{:S(2)}) copy-start(f32[1,1024]{1,0:T(1,128)} %get-tuple-element.169) | copy-start | bytes 12292
  575.8 41.2 %copy-start.51 = (f32[128]{0:T(128)S(1)}, f32[128]{0:T(128)}, u32[]{:S(2)}) copy-start(f32[128]{0:T(128)} %copy-done.50) | copy-start | bytes 1540
  575.8 41.2 %copy-start.54 = (f32[128]{0:T(128)S(1)}, f32[128]{0:T(128)}, u32[]{:S(2)}) copy-start(f32[128]{0:T(128)} %copy-done.53) | copy-start | bytes 1540
  578.4 287.5 %reduce-scatter.25.cloned.1.call-start = ((), (), s32[]{:S(2)}) async-start(), calls=%async_computation.20 | async-start | bytes 540672
  617.0 6.1 copy-start.23
  617.0 6.2 copy-start.39
  617.0 7.3 copy-start.8
  617.0 7.3 copy-start.17
  624.3 382.1 %reduce-scatter.19.cloned.1.call-start = ((), (), s32[]{:S(2)}) async-start(), calls=%async_computation.17 | async-start | bytes 4325376 | tf_op jit(solution)/shard_map/reduce_scatter | solution.py:254
  627.1 558.1 %reduce-scatter.17.cloned.1.call-start = ((), (), s32[]{:S(2)}) async-start(), calls=%async_computation.16 | async-start | bytes 12976128 | tf_op jit(solution)/shard_map/reduce_scatter | solution.py:253
  634.4 740.6 %reduce-scatter.21.cloned.1.call-start = ((), (), s32[]{:S(2)}) async-start(), calls=%async_computation.18 | async-start | bytes 17301504 | tf_op jit(solution)/shard_map/reduce_scatter | solution.py:186
  643.8 3.0 copy-start.42
  643.9 42.4 %copy-start.49 = (f32[2,128]{1,0:T(2,128)S(1)}, f32[2,128]{1,0:T(2,128)}, u32[]{:S(2)}) copy-start(f32[2,128]{1,0:T(2,128)} %param.33) | copy-start | bytes 3076
  643.9 42.5 %copy-start.60 = (f32[128]{0:T(128)S(1)}, f32[128]{0:T(128)}, u32[]{:S(2)}) copy-start(f32[128]{0:T(128)} %param.26) | copy-start | bytes 1540
  643.9 43.6 %copy-start.2 = (f32[128,4096]{1,0:T(8,128)S(1)}, f32[128,4096]{1,0:T(8,128)}, u32[]{:S(2)}) copy-start(f32[128,4096]{1,0:T(8,128)} %copy-done.1) | copy-start | bytes 6291460
  643.9 43.6 %copy-start.47 = (f32[1,1024]{1,0:T(1,128)S(1)}, f32[1,1024]{1,0:T(1,128)}, u32[]{:S(2)}) copy-start(f32[1,1024]{1,0:T(1,128)} %get-tuple-element.176) | copy-start | bytes 12292
  686.4 6.9 copy-start.58
  687.5 44.9 %copy-start.45 = (f32[3,32]{1,0:T(4,128)S(1)}, f32[3,32]{1,0:T(4,128)}, u32[]{:S(2)}) copy-start(f32[3,32]{1,0:T(4,128)} %param.25) | copy-start | bytes 1156
  687.5 46.1 %copy-start.38 = (f32[1,1024]{1,0:T(1,128)S(1)}, f32[1,1024]{1,0:T(1,128)}, u32[]{:S(2)}) copy-start(f32[1,1024]{1,0:T(1,128)} %get-tuple-element.169) | copy-start | bytes 12292
  687.5 46.1 %copy-start.52 = (f32[128]{0:T(128)S(1)}, f32[128]{0:T(128)}, u32[]{:S(2)}) copy-start(f32[128]{0:T(128)} %copy-done.50) | copy-start | bytes 1540
  687.5 46.1 %copy-start.55 = (f32[128]{0:T(128)S(1)}, f32[128]{0:T(128)}, u32[]{:S(2)}) copy-start(f32[128]{0:T(128)} %copy-done.53) | copy-start | bytes 1540
  693.3 41.9 %copy-start.25 = (f32[128,1024]{1,0:T(8,128)S(1)}, f32[128,1024]{1,0:T(8,128)}, u32[]{:S(2)}) copy-start(f32[128,1024]{1,0:T(8,128)} %fusion.8) | copy-start | bytes 1572868
  693.3 41.9 %copy-start.57 = (f32[2]{0:T(128)S(1)}, f32[2]{0:T(128)}, u32[]{:S(2)}) copy-start(f32[2]{0:T(128)} %copy-done.56) | copy-start | bytes 28
  732.4 3.9 copy-start.43
  733.6 133.1 %copy-start.41 = (f32[5,32]{1,0:T(8,128)S(1)}, f32[5,32]{1,0:T(8,128)}, u32[]{:S(2)}) copy-start(f32[5,32]{1,0:T(8,128)} %param.22) | copy-start | bytes 1924
  733.6 272.8 %copy-start.29 = (f32[2,32,1024]{2,1,0:T(8,128)S(1)}, f32[2,32,1024]{2,1,0:T(8,128)}, u32[]{:S(2)}) copy-start(f32[2,32,1024]{2,1,0:T(8,128)} %param.28) | copy-start | bytes 786436
  735.1 450.2 %copy-start.20 = (f32[32,3072]{1,0:T(8,128)S(1)}, f32[32,3072]{1,0:T(8,128)}, u32[]{:S(2)}) copy-start(f32[32,3072]{1,0:T(8,128)} %param.20) | copy-start | bytes 1179652
  735.1 450.2 %copy-start.24 = (f32[2,32,3072]{2,1,0:T(8,128)S(1)}, f32[2,32,3072]{2,1,0:T(8,128)}, u32[]{:S(2)}) copy-start(f32[2,32,3072]{2,1,0:T(8,128)} %param.27) | copy-start | bytes 2359300
  866.7 320.6 %copy-start.40 = (f32[32,5]{0,1:T(8,128)}, f32[32,5]{0,1:T(8,128)S(1)}, u32[]{:S(2)}) copy-start(f32[32,5]{0,1:T(8,128)S(1)} %copy.118) | copy-start | bytes 1924
  1008.8 366.2 %copy-start.19 = (f32[32,4096]{1,0:T(8,128)S(1)}, f32[32,4096]{1,0:T(8,128)}, u32[]{:S(2)}) copy-start(f32[32,4096]{1,0:T(8,128)} %param.23) | copy-start | bytes 1572868
  1008.8 366.2 %copy-start.22 = (f32[2,32,4096]{2,1,0:T(8,128)S(1)}, f32[2,32,4096]{2,1,0:T(8,128)}, u32[]{:S(2)}) copy-start(f32[2,32,4096]{2,1,0:T(8,128)} %param.30) | copy-start | bytes 3145732
  (12 other events, 11.4 us)
Sparse Core Ops, SparseCore 0:
  11.5 70.9 all-gather.9
  87.3 15.2 all-gather.11
  104.7 16.6 all-gather.13
  124.7 55.3 all-gather.15
  183.4 76.9 all-gather.17
  274.8 183.8 reduce-scatter.22
  462.1 76.4 all-gather.19
  566.8 22.7 reduce-scatter.14
  592.2 24.7 reduce-scatter.12
  619.1 112.4 reduce-scatter.26
  734.4 131.4 reduce-scatter.24
  868.6 137.7 reduce-scatter.18
  1013.0 172.2 reduce-scatter.16
  1188.0 186.9 reduce-scatter.20
where the time goes:
time: 1390 us; the launch traced here: 1380 us
  waiting for transfers between devices  1080 us (78%)
  blocking collectives  145 us (10%)
  matrix products  74.3 us (5%)
  local copies, waits for them, and re-layouts  34.1 us (2%)
  other arithmetic  33.4 us (2%)
  between operations  14.6 us (1%)
    reduce_scatter x1, waiting for transfers between devices, body(): lax.psum_scatter(expand_grad, ('dp', 'seq'), scatter_dimension=0, tiled=T...  187 us
    reduce_scatter x1, waiting for transfers between devices, body(): lax.psum_scatter(shrink_grad, ('dp', 'seq'), scatter_dimension=0, tiled=T...  184 us
    reduce_scatter x1, waiting for transfers between devices, body(): lax.psum_scatter(inward_grad, ('dp', 'seq'), scatter_dimension=0, tiled=T...  176 us
    unnamed x16, waiting for transfers between devices  168 us
    reduce_scatter x1, waiting for transfers between devices, body(): lax.psum_scatter(outward_grad, ('dp', 'seq'), scatter_dimension=0, tiled=...  138 us
    all_gather x1, waiting for transfers between devices, body(): lax.all_gather(halved(expand), ('dp', 'seq'), axis=0, tiled=True)  77.8 us
    all_gather x1, waiting for transfers between devices, body(): lax.all_gather(halved(shrink), ('dp', 'seq'), axis=0, tiled=True)  75.1 us
    unnamed x1, blocking collectives  39.5 us
  transfers between devices with their start and end apart: 14, of which 12 were waited for; matrix products, arithmetic and copies ran while one was open for 6% of the time, Pallas kernels for 0%

commit v1 on v0

--- a/solution.py
+++ b/solution.py
@@ -16,6 +16,18 @@
 gelu_scale = 0.7978845608028654
 gelu_cubic = 0.044715
 masked_score = -1e30
+
+
+def gather_by_bits(x, axis, dim):
+    ways, here = (lax.axis_size(axis), lax.axis_index(axis))
+    grown, reach = (x, 1)
+    while reach < ways:
+        theirs = lax.ppermute(grown, axis, [(d, d ^ reach) for d in range(ways)])
+        mine_first = jnp.concatenate([grown, theirs], axis=dim)
+        theirs_first = jnp.concatenate([theirs, grown], axis=dim)
+        grown = jnp.where(here & reach == 0, mine_first, theirs_first)
+        reach = 2 * reach
+    return grown
 
 
 def halved(operand):
@@ -142,7 +154,7 @@
     upper_raw, lifted_two, vec_rows_two = lifted_fold(
         normed_two,
         (
-            lax.all_gather(halved(expand), ("dp", "seq"), axis=0, tiled=True),
+            gather_by_bits(halved(expand), ("dp", "seq"), 0),
             lax.all_gather(feed_cols, ("dp", "seq"), axis=0, tiled=True),
         ),
     )

time: 1390 us -> 1620 us (1.17)
  blocking collectives: 145 us -> 315 us
  waiting for transfers between devices: 1080 us -> 1120 us
    all_gather x1, blocking collectives: 33 us -> 209 us  [body(): lax.all_gather(feed_cols, ('dp', 'seq'), axis=0, tiled=True)]
    ppermute x0 -> x5, waiting for transfers between devices: none -> 54 us  [gather_by_bits(): theirs = lax.ppermute(grown, axis, [(d, d ^ reach) for d in range(ways)])]
  transfers between devices with their start and end apart: 14 -> 19, of which waited for: 12 -> 13; matrix products, arithmetic and copies ran while one was open for 6% -> 6% of each run, Pallas kernels for 0% -> 0%
where the time goes in v1:
time: 1620 us; the launch traced here: 1610 us
  waiting for transfers between devices  1120 us (69%)
  blocking collectives  315 us (19%)
  matrix products  78.5 us (5%)
  other arithmetic  38.2 us (2%)
  local copies, waits for them, and re-layouts  36.9 us (2%)
    all_gather x1, blocking collectives, body(): lax.all_gather(feed_cols, ('dp', 'seq'), axis=0, tiled=True)  209 us
    reduce_scatter x1, waiting for transfers between devices, body(): lax.psum_scatter(shrink_grad, ('dp', 'seq'), scatter_dimension=0, tiled=T...  188 us
    reduce_scatter x1, waiting for transfers between devices, body(): lax.psum_scatter(expand_grad, ('dp', 'seq'), scatter_dimension=0, tiled=T...  187 us
    reduce_scatter x1, waiting for transfers between devices, body(): lax.psum_scatter(inward_grad, ('dp', 'seq'), scatter_dimension=0, tiled=T...  177 us
    unnamed x16, waiting for transfers between devices  171 us
    reduce_scatter x1, waiting for transfers between devices, body(): lax.psum_scatter(outward_grad, ('dp', 'seq'), scatter_dimension=0, tiled=...  138 us
    all_gather x1, waiting for transfers between devices, body(): lax.all_gather(halved(shrink), ('dp', 'seq'), axis=0, tiled=True)  74.2 us
    all_gather x1, waiting for transfers between devices, body(): lax.all_gather(halved(expand), ('dp', 'seq'), axis=0, tiled=True)  70 us
  transfers between devices with their start and end apart: 19, of which 13 were waited for; matrix products, arithmetic and copies ran while one was open for 6% of the time, Pallas kernels for 0%

profile of v1, /device:TPU:9, one launch (start us, length us, event | category | flops | bytes accessed | tf_op | source)
XLA Modules:
  0.0 1614.5 jit_solution(2311156718169087570)
XLA Ops:
  7.3 1.7 convert_element_type.120
  9.1 1.1 convert_element_type.131
  10.9 1.1 reduce_sum.171
  12.1 35.6 %all-gather = bf16[32,32,5]{1,2,0:T(8,128)(2,1)S(1)} all-gather(bf16[1,32,5]{1,2,0:T(8,128)(2,1)S(1)} %convert_bitcast_fusion), channel_id=1, replica_groups=mesh['dp'=8,'seq'=4] {'dp','seq'}, dimensions={0}, use_global_device_ids=true | all-gather | bytes 10560 | tf_op jit(solution)/shard_map/all_gather | solution.py:113
  49.2 13.5 collective-permute-done.1
  63.0 26.4 %all-gather.10.cloned.1.call-done = bf16[1024,3072]{1,0:T(8,128)(2,1)} async-done(((bf16[32,3072]{1,0:T(8,128)(2,1)}), bf16[1024,3072]{1,0:T(8,128)(2,1)}) %all-gather.10.cloned.1.call-update) | async-done | bytes 6291472 | tf_op jit(solution)/shard_map/all_gather | solution.py:112
  89.4 3.8 fusion.70
  93.2 1.2 copy-done.8
  95.3 3.1 maximum_select_fusion.5
  98.3 3.7 collective-permute-start.3
  102.0 1.8 slice.181
  104.7 40.5 %collective-permute-done.3 = bf16[256,4096]{1,0:T(8,128)(2,1)} collective-permute-done((bf16[256,4096]{1,0:T(8,128)(2,1)S(1)}, bf16[256,4096]{1,0:T(8,128)(2,1)}, u32[]{:S(2)}, u32[]{:S(2)}) %collective-permute-start.3) | collective-permute-done | bytes 2097184 | tf_op jit(solution)/shard_map/ppermute | solution.py:25
  145.2 4.9 maximum_select_fusion.4
  150.1 1.6 collective-permute-start.4
  151.8 208.6 %all-gather.1 = bf16[32,32,3]{1,2,0:T(4,128)(2,1)S(1)} all-gather(bf16[1,32,3]{1,2,0:T(4,128)(2,1)S(1)} %convert_bitcast_fusion.1), channel_id=1, replica_groups=mesh['dp'=8,'seq'=4] {'dp','seq'}, dimensions={0}, use_global_device_ids=true | all-gather | bytes 6336 | tf_op jit(solution)/shard_map/all_gather | solution.py:158
  360.5 32.0 %all-gather.2 = bf16[32,1,128]{2,1,0:T(2,128)(2,1)S(1)} all-gather(bf16[1,1,128]{2,1,0:T(2,128)(2,1)S(1)} %convert_bitcast_fusion.2), channel_id=1, replica_groups=mesh['dp'=8,'seq'=4] {'dp','seq'}, dimensions={0}, use_global_device_ids=true | all-gather | bytes 8448 | tf_op jit(solution)/shard_map/all_gather | solution.py:163
  394.0 1.8 fusion.59
  398.2 2.4 copy.101
  400.6 2.3 copy.102
  402.9 1.9 fusion.67
  406.1 1.2 copy.104
  407.3 2.1 convert_element_type.126
  409.4 2.1 fusion.68
  411.8 7.6 fusion.7
  419.4 1.4 copy-done.16
  420.8 8.2 fusion.58
  429.1 187.7 %reduce-scatter.23.cloned.1.call-done = f32[128,1024]{1,0:T(8,128)} async-done(((f32[4096,1024]{1,0:T(8,128)}), f32[128,1024]{1,0:T(8,128)}) %reduce-scatter.23.cloned.1.call-update) | async-done | bytes 524304 | tf_op jit(solution)/shard_map/reduce_scatter | solution.py:199
  616.7 3.3 fusion.32
  621.1 1.4 fusion.64
  622.5 74.2 %all-gather.18.cloned.1.call-done = bf16[4096,1024]{1,0:T(8,128)(2,1)} async-done(((bf16[128,1024]{1,0:T(8,128)(2,1)}), bf16[4096,1024]{1,0:T(8,128)(2,1)}) %all-gather.18.cloned.1.call-update) | async-done | bytes 8388624 | tf_op jit(solution)/shard_map/all_gather | solution.py:162
  696.7 9.1 fusion.69
  705.8 70.0 %all-gather.20.cloned.1.call-done = bf16[1024,4096]{1,0:T(8,128)(2,1)} async-done(((bf16[32,4096]{1,0:T(8,128)(2,1)}), bf16[1024,4096]{1,0:T(8,128)(2,1)}) %all-gather.20.cloned.1.call-update) | async-done | bytes 8388624 | tf_op jit(solution)/shard_map/all_gather | solution.py:190
  775.8 7.3 multiply_reduce_fusion.1
  784.8 1.5 convolution_convert_fusion.3
  786.4 2.1 reshape.220
  788.5 2.2 copy.107
  790.8 2.6 convolution_convert_fusion
  793.4 2.3 copy.112
  795.7 1.4 multiply_reduce_fusion
  797.1 2.3 multiply_convert_fusion
  800.4 1.4 convolution_convert_fusion.1
  801.8 2.4 copy.110
  806.3 1.0 copy.119
  807.7 10.9 reduce-scatter.15.cloned.1.call-done
  818.6 27.4 %reduce-scatter.13.cloned.1.call-done = bf16[2,64,1024]{2,1,0:T(8,128)(2,1)} async-done(((bf16[2,256,1024]{2,1,0:T(8,128)(2,1)}), bf16[2,64,1024]{2,1,0:T(8,128)(2,1)}) %reduce-scatter.13.cloned.1.call-update) | async-done | bytes 262160 | tf_op jit(solution)/shard_map/reduce_scatter | solution.py:239
  846.0 5.9 multiply_reduce_fusion.2
  852.0 1.0 copy.117
  853.1 2.7 fusion.34
  856.8 6.4 fusion.27
  863.3 1.1 copy-done.14
  864.5 8.3 fusion.22
  874.0 1.0 pad_maximum_fusion.1
  875.0 38.7 %all-reduce = f32[4096]{0:T(1024)S(1)} all-reduce(f32[4096]{0:T(1024)S(1)} %copy-done.45), channel_id=10, replica_groups=mesh['dp'=8,'seq'=4] {'dp','seq'}, use_global_device_ids=true, to_apply=%region_29.30.clone | all-reduce | flops 4096 | bytes 32768
  915.0 6.4 fusion.16
  921.4 39.6 %reduce-scatter.27.cloned.1.call-done = f32[32,3]{1,0:T(8,128)} async-done(((f32[1024,3]{1,0:T(8,128)}), f32[32,3]{1,0:T(8,128)}) %reduce-scatter.27.cloned.1.call-update) | async-done | bytes 400
  963.4 1.2 broadcast_multiply_fusion
  964.5 130.9 %reduce-scatter.25.cloned.1.call-done = f32[32,5]{1,0:T(8,128)} async-done(((f32[1024,5]{1,0:T(8,128)}), f32[32,5]{1,0:T(8,128)}) %reduce-scatter.25.cloned.1.call-update) | async-done | bytes 656
  1097.5 138.4 %reduce-scatter.19.cloned.1.call-done = f32[32,1024]{1,0:T(8,128)} async-done(((f32[1024,1024]{1,0:T(8,128)}), f32[32,1024]{1,0:T(8,128)}) %reduce-scatter.19.cloned.1.call-update) | async-done | bytes 131088 | tf_op jit(solution)/shard_map/reduce_scatter | solution.py:266
  1235.9 1.7 fusion.41
  1238.3 176.7 %reduce-scatter.17.cloned.1.call-done = f32[32,3072]{1,0:T(8,128)} async-done(((f32[1024,3072]{1,0:T(8,128)}), f32[32,3072]{1,0:T(8,128)}) %reduce-scatter.17.cloned.1.call-update) | async-done | bytes 393232 | tf_op jit(solution)/shard_map/reduce_scatter | solution.py:265
  1415.0 2.1 fusion.39
  1418.0 186.7 %reduce-scatter.21.cloned.1.call-done = f32[32,4096]{1,0:T(8,128)} async-done(((f32[1024,4096]{1,0:T(8,128)}), f32[32,4096]{1,0:T(8,128)}) %reduce-scatter.21.cloned.1.call-update) | async-done | bytes 524304 | tf_op jit(solution)/shard_map/reduce_scatter | solution.py:198
  1604.7 2.2 fusion.31
  1606.9 1.0 pad_maximum_fusion
  (244 shorter events, 25.3 us)
Async XLA Ops:
  7.2 40.5 %copy-start = (f32[2,64,1024]{2,1,0:T(8,128)S(1)}, f32[2,64,1024]{2,1,0:T(8,128)}, u32[]{:S(2)}) copy-start(f32[2,64,1024]{2,1,0:T(8,128)} %param.17) | copy-start | bytes 1572868
  7.2 4.9 copy-start.43
  7.2 82.2 %all-gather.10.cloned.1.call-start = ((), (), s32[]{:S(2)}) async-start(), calls=%async_computation.8 | async-start | bytes 6488064 | tf_op jit(solution)/shard_map/all_gather | solution.py:112
  9.0 389.1 %all-gather.12.cloned.1.call-start = ((), (), s32[]{:S(2)}) async-start(), calls=%async_computation.9 | async-start | bytes 1310720 | tf_op jit(solution)/shard_map/all_gather | solution.py:128
  10.2 39.0 %copy-start.18 = (bf16[32,4096]{1,0:T(8,128)(2,1)}, bf16[32,4096]{1,0:T(8,128)(2,1)S(1)}, u32[]{:S(2)}) copy-start(bf16[32,4096]{1,0:T(8,128)(2,1)S(1)} %convert_element_type.131) | copy-start | bytes 786436
  10.2 37.9 %collective-permute-start = (bf16[32,4096]{1,0:T(8,128)(2,1)S(1)}, bf16[32,4096]{1,0:T(8,128)(2,1)S(1)}, u32[]{:S(2)}, u32[]{:S(2)}) collective-permute-start(bf16[32,4096]{1,0:T(8,128)(2,1)S(1)} %convert_element_type.131), channel_id=1, source_target_pairs={{0,1},{1,0},{2,3},{3,2},{4,5},{5,4},{6,7},{7,6},{8,9},{9,8},{10,11... | collective-permute-start | bytes 786440 | tf_op jit(solution)/shard_map/ppermute | solution.py:25
  48.1 14.5 collective-permute-start.1
  48.3 44.8 %copy-start.60 = (f32[128]{0:T(128)}, f32[128]{0:T(128)S(1)}, u32[]{:S(2)}) copy-start(f32[128]{0:T(128)S(1)} %div.132) | copy-start | bytes 1540
  48.4 44.8 %copy-start.63 = (f32[128]{0:T(128)}, f32[128]{0:T(128)S(1)}, u32[]{:S(2)}) copy-start(f32[128]{0:T(128)S(1)} %rsqrt.20) | copy-start | bytes 1540
  62.9 30.3 %copy-start.15 = (bf16[128,4096]{1,0:T(8,128)(2,1)}, bf16[128,4096]{1,0:T(8,128)(2,1)S(1)}, u32[]{:S(2)}) copy-start(bf16[128,4096]{1,0:T(8,128)(2,1)S(1)} %maximum_select_fusion.6) | copy-start | bytes 3145732
  62.9 32.4 %collective-permute-start.2 = (bf16[128,4096]{1,0:T(8,128)(2,1)S(1)}, bf16[128,4096]{1,0:T(8,128)(2,1)}, u32[]{:S(2)}, u32[]{:S(2)}) collective-permute-start(bf16[128,4096]{1,0:T(8,128)(2,1)S(1)} %maximum_select_fusion.6), channel_id=1, source_target_pairs={{0,4},{1,5},{2,6},{3,7},{4,0},{5,1},{6,2},{7,3},{8,12},{9,13},{10,... | collective-permute-start | bytes 3145736 | tf_op jit(solution)/shard_map/ppermute | solution.py:25
  95.2 305.4 %all-gather.14.cloned.1.call-start = ((), (), s32[]{:S(2)}) async-start(), calls=%async_computation.10 | async-start | bytes 1310720 | tf_op jit(solution)/shard_map/all_gather | solution.py:127
  95.2 8.7 copy-start.28
  98.3 46.9 %collective-permute-start.3 = (bf16[256,4096]{1,0:T(8,128)(2,1)S(1)}, bf16[256,4096]{1,0:T(8,128)(2,1)}, u32[]{:S(2)}, u32[]{:S(2)}) collective-permute-start(bf16[256,4096]{1,0:T(8,128)(2,1)S(1)} %maximum_select_fusion.5), channel_id=1, source_target_pairs={{0,8},{1,9},{2,10},{3,11},{4,12},{5,13},{6,14},{7,15},{8,0},{9,1},... | collective-permute-start | bytes 6291464 | tf_op jit(solution)/shard_map/ppermute | solution.py:25
  103.9 305.5 %all-gather.16.cloned.1.call-start = ((), (), s32[]{:S(2)}) async-start(), calls=%async_computation.11 | async-start | bytes 2162688 | tf_op jit(solution)/shard_map/all_gather | solution.py:149
  104.6 512.2 %reduce-scatter.23.cloned.1.call-start = ((), (), s32[]{:S(2)}) async-start(), calls=%async_computation.19 | async-start | bytes 17301504 | tf_op jit(solution)/shard_map/reduce_scatter | solution.py:199
  104.6 47.1 %copy-start.54 = (f32[3,32]{1,0:T(4,128)S(1)}, f32[3,32]{1,0:T(4,128)}, u32[]{:S(2)}) copy-start(f32[3,32]{1,0:T(4,128)} %param.25) | copy-start | bytes 1156
  104.6 255.8 %copy-start.69 = (f32[128]{0:T(128)S(1)}, f32[128]{0:T(128)}, u32[]{:S(2)}) copy-start(f32[128]{0:T(128)} %param.26) | copy-start | bytes 1540
  104.7 288.4 %copy-start.71 = (s32[8]{0:T(128)S(1)}, s32[8]{0:T(128)}, u32[]{:S(2)}) copy-start(s32[8]{0:T(128)} %param.19) | copy-start | bytes 100
  150.1 261.7 %collective-permute-start.4 = (bf16[512,4096]{1,0:T(8,128)(2,1)}, bf16[512,4096]{1,0:T(8,128)(2,1)}, u32[]{:S(2)}, u32[]{:S(2)}) collective-permute-start(bf16[512,4096]{1,0:T(8,128)(2,1)} %maximum_select_fusion.4), channel_id=1, source_target_pairs={{0,16},{1,17},{2,18},{3,19},{4,20},{5,21},{6,22},{7,23},{8,24},{9,... | collective-permute-start | bytes 12582920 | tf_op jit(solution)/shard_map/ppermute | solution.py:25
  360.4 40.2 %copy-start.35 = (f32[1024,3]{0,1:T(4,128)}, f32[1024,3]{0,1:T(4,128)S(1)}, u32[]{:S(2)}) copy-start(f32[1024,3]{0,1:T(4,128)S(1)} %reshape.232) | copy-start | bytes 36868
  393.3 7.3 copy-start.66
  398.1 4.8 copy-start.9
  411.6 7.8 copy-start.47
  411.8 7.6 copy-start.50
  411.8 9.0 copy-start.23
  429.0 267.7 %all-gather.18.cloned.1.call-start = ((), (), s32[]{:S(2)}) async-start(), calls=%async_computation.12 | async-start | bytes 8650752 | tf_op jit(solution)/shard_map/all_gather | solution.py:162
  620.0 155.8 %all-gather.20.cloned.1.call-start = ((), (), s32[]{:S(2)}) async-start(), calls=%async_computation.13 | async-start | bytes 8650752 | tf_op jit(solution)/shard_map/all_gather | solution.py:190
  620.8 197.8 %reduce-scatter.15.cloned.1.call-start = ((), (), s32[]{:S(2)}) async-start(), calls=%async_computation.15 | async-start | bytes 1310720 | tf_op jit(solution)/shard_map/reduce_scatter | solution.py:242
  775.8 7.4 copy-start.12
  775.8 7.4 copy-start.36
  775.8 7.4 copy-start.48
  775.8 7.4 copy-start.51
  795.6 50.3 %reduce-scatter.13.cloned.1.call-start = ((), (), s32[]{:S(2)}) async-start(), calls=%async_computation.14 | async-start | bytes 1310720 | tf_op jit(solution)/shard_map/reduce_scatter | solution.py:239
  804.3 156.7 %reduce-scatter.27.cloned.1.call-start = ((), (), s32[]{:S(2)}) async-start(), calls=%async_computation.21 | async-start | bytes 540672
  804.8 41.2 %copy-start.39 = (f32[1,1024]{1,0:T(1,128)S(1)}, f32[1,1024]{1,0:T(1,128)}, u32[]{:S(2)}) copy-start(f32[1,1024]{1,0:T(1,128)} %get-tuple-element.169) | copy-start | bytes 12292
  804.8 41.2 %copy-start.61 = (f32[128]{0:T(128)S(1)}, f32[128]{0:T(128)}, u32[]{:S(2)}) copy-start(f32[128]{0:T(128)} %copy-done.60) | copy-start | bytes 1540
  804.8 41.1 %copy-start.64 = (f32[128]{0:T(128)S(1)}, f32[128]{0:T(128)}, u32[]{:S(2)}) copy-start(f32[128]{0:T(128)} %copy-done.63) | copy-start | bytes 1540
  807.4 288.1 %reduce-scatter.25.cloned.1.call-start = ((), (), s32[]{:S(2)}) async-start(), calls=%async_computation.20 | async-start | bytes 540672
  846.0 6.0 copy-start.25
  846.0 6.0 copy-start.41
  846.0 7.1 copy-start.6
  846.0 7.1 copy-start.17
  853.1 382.8 %reduce-scatter.19.cloned.1.call-start = ((), (), s32[]{:S(2)}) async-start(), calls=%async_computation.17 | async-start | bytes 4325376 | tf_op jit(solution)/shard_map/reduce_scatter | solution.py:266
  855.9 559.1 %reduce-scatter.17.cloned.1.call-start = ((), (), s32[]{:S(2)}) async-start(), calls=%async_computation.16 | async-start | bytes 12976128 | tf_op jit(solution)/shard_map/reduce_scatter | solution.py:265
  863.3 741.4 %reduce-scatter.21.cloned.1.call-start = ((), (), s32[]{:S(2)}) async-start(), calls=%async_computation.18 | async-start | bytes 17301504 | tf_op jit(solution)/shard_map/reduce_scatter | solution.py:198
  872.8 41.0 %copy-start.59 = (f32[2,128]{1,0:T(2,128)S(1)}, f32[2,128]{1,0:T(2,128)}, u32[]{:S(2)}) copy-start(f32[2,128]{1,0:T(2,128)} %param.33) | copy-start | bytes 3076
  872.8 41.0 %copy-start.70 = (f32[128]{0:T(128)S(1)}, f32[128]{0:T(128)}, u32[]{:S(2)}) copy-start(f32[128]{0:T(128)} %param.26) | copy-start | bytes 1540
  872.8 42.1 %copy-start.57 = (f32[1,1024]{1,0:T(1,128)S(1)}, f32[1,1024]{1,0:T(1,128)}, u32[]{:S(2)}) copy-start(f32[1,1024]{1,0:T(1,128)} %get-tuple-element.176) | copy-start | bytes 12292
  913.8 7.6 copy-start.68
  914.9 46.9 %copy-start.55 = (f32[3,32]{1,0:T(4,128)S(1)}, f32[3,32]{1,0:T(4,128)}, u32[]{:S(2)}) copy-start(f32[3,32]{1,0:T(4,128)} %param.25) | copy-start | bytes 1156
  914.9 48.1 %copy-start.73 = (f32[128]{0:T(128)S(1)}, f32[128]{0:T(128)}, u32[]{:S(2)}) copy-start(f32[128]{0:T(128)} %get-tuple-element.141) | copy-start | bytes 1540
  914.9 48.1 %copy-start.72 = (f32[128]{0:T(128)S(1)}, f32[128]{0:T(128)}, u32[]{:S(2)}) copy-start(f32[128]{0:T(128)} %get-tuple-element.142) | copy-start | bytes 1540
  914.9 48.1 %copy-start.40 = (f32[1,1024]{1,0:T(1,128)S(1)}, f32[1,1024]{1,0:T(1,128)}, u32[]{:S(2)}) copy-start(f32[1,1024]{1,0:T(1,128)} %get-tuple-element.169) | copy-start | bytes 12292
  914.9 48.1 %copy-start.62 = (f32[128]{0:T(128)S(1)}, f32[128]{0:T(128)}, u32[]{:S(2)}) copy-start(f32[128]{0:T(128)} %copy-done.60) | copy-start | bytes 1540
  915.0 48.1 %copy-start.65 = (f32[128]{0:T(128)S(1)}, f32[128]{0:T(128)}, u32[]{:S(2)}) copy-start(f32[128]{0:T(128)} %copy-done.63) | copy-start | bytes 1540
  921.4 42.0 %copy-start.67 = (f32[2]{0:T(128)S(1)}, f32[2]{0:T(128)}, u32[]{:S(2)}) copy-start(f32[2]{0:T(128)} %copy-done.66) | copy-start | bytes 28
  963.1 133.2 %copy-start.44 = (f32[5,32]{1,0:T(8,128)S(1)}, f32[5,32]{1,0:T(8,128)}, u32[]{:S(2)}) copy-start(f32[5,32]{1,0:T(8,128)} %param.22) | copy-start | bytes 1924
  963.1 272.8 %copy-start.29 = (f32[2,32,1024]{2,1,0:T(8,128)S(1)}, f32[2,32,1024]{2,1,0:T(8,128)}, u32[]{:S(2)}) copy-start(f32[2,32,1024]{2,1,0:T(8,128)} %param.28) | copy-start | bytes 786436
  963.3 451.7 %copy-start.22 = (f32[32,3072]{1,0:T(8,128)S(1)}, f32[32,3072]{1,0:T(8,128)}, u32[]{:S(2)}) copy-start(f32[32,3072]{1,0:T(8,128)} %param.20) | copy-start | bytes 1179652
  963.3 451.7 %copy-start.26 = (f32[2,32,3072]{2,1,0:T(8,128)S(1)}, f32[2,32,3072]{2,1,0:T(8,128)}, u32[]{:S(2)}) copy-start(f32[2,32,3072]{2,1,0:T(8,128)} %param.27) | copy-start | bytes 2359300
  1096.2 320.8 %copy-start.42 = (f32[32,5]{0,1:T(8,128)}, f32[32,5]{0,1:T(8,128)S(1)}, u32[]{:S(2)}) copy-start(f32[32,5]{0,1:T(8,128)S(1)} %copy.118) | copy-start | bytes 1924
  1238.3 366.4 %copy-start.19 = (f32[32,4096]{1,0:T(8,128)S(1)}, f32[32,4096]{1,0:T(8,128)}, u32[]{:S(2)}) copy-start(f32[32,4096]{1,0:T(8,128)} %param.23) | copy-start | bytes 1572868
  1238.3 366.4 %copy-start.24 = (f32[2,32,4096]{2,1,0:T(8,128)S(1)}, f32[2,32,4096]{2,1,0:T(8,128)}, u32[]{:S(2)}) copy-start(f32[2,32,4096]{2,1,0:T(8,128)} %param.30) | copy-start | bytes 3145732
  (29 other events, 48.3 us)
Sparse Core Ops, SparseCore 0:
  11.5 77.8 all-gather.9
  95.3 16.8 all-gather.11
  114.4 16.6 all-gather.13
  134.4 222.5 all-gather.15
  429.1 187.5 reduce-scatter.22
  620.2 76.4 all-gather.17
  700.1 75.6 all-gather.19
  795.8 22.7 reduce-scatter.14
  821.1 24.7 reduce-scatter.12
  848.6 112.3 reduce-scatter.26
  963.8 131.5 reduce-scatter.24
  1098.1 137.7 reduce-scatter.18
  1242.5 172.4 reduce-scatter.16
  1417.7 186.9 reduce-scatter.20
